TPU v7x, 32 devices: a whole 2x2x4 slice. The times are simulated.
32 devices in a mesh: dp: 4 (over y, x), expert: 4 (over z), tensor: 2 (over core).
Axes of the slice: x: 2, y: 2, z: 4, core: 2. Of those that a mesh axis runs over, the one named last changes fastest.
Arguments:
- tokens: bfloat16 [2048, 2048], P(('dp', 'expert'), 'tensor'), may hold values from -6 to 6
- norm_gain: bfloat16 [2048], replicated, may hold values from 0.25 to 1.75
- expert_ids: int32 [2048, 2], P(('dp', 'expert')), may hold values from 0 to 3, all different within a row; in each aligned block of 128 rows (0 to 127, 128 to 255, ...) at most 128 rows name the same one
- gate_codes: int32 [2048, 2], P(('dp', 'expert')), may hold values from 1 to 255
- gate_weights: bfloat16 [4, 7168, 2048], P('expert', ('dp', 'tensor')), may hold values from -0.125 to 0.125
- up_weights: bfloat16 [4, 7168, 2048], P('expert', ('dp', 'tensor')), may hold values from -0.125 to 0.125
- down_weights: bfloat16 [4, 7168, 2048], P('expert', ('dp', 'tensor')), may hold values from -0.0625 to 0.0625
- value_head: bfloat16 [2048, 128], replicated, may hold values from -0.125 to 0.125
- actions: int32 [2048], P(('dp', 'expert')), may hold values from 0 to 127
- rewards: int32 [2048], P(('dp', 'expert')), may hold values from -8 to 8
- trace_codes: int32 [2048], P(('dp', 'expert')), may hold values from 1 to 1024
Outputs:
- action_values: float32 [2048, 128], P(('dp', 'expert'))
- retrace_targets: float32 [2048], P(('dp', 'expert'))
Inputs may be any that keep to these rules, and one draw needn't show every extreme that they name: `expert_ids`: each row names 2 different experts; within the 128 rows of one index pair of dp and expert each expert is named by at most 128 rows, and in some of these blocks one expert by exactly 128.
All inputs are finite; a program needn't handle non-finite values.
Results may differ from a plain program's by a relative error of at most 0.005.
Values may be sent and summed in bfloat16 or wider, within the bound.
No kernel may reach another device: no remote copies, remote signals or barrier semaphores. Data moves between devices by JAX's collectives and lax.ppermute only.
A program may use at most 256 MiB of HBM per device.

v0:
```python
import jax
import jax.numpy as jnp
from jax import lax
from jax.sharding import PartitionSpec as P

TOP = 2
STEPS = 128
DISCOUNT = 0.99
EPSILON = 1e-05


def expert_rows(row_block, gate_matrix, lift_matrix, down_matrix):
    gate_value = lax.dot_general(
        row_block, gate_matrix, (((1,), (1,)), ((), ())), preferred_element_type=jnp.float32
    )
    lift_value = lax.dot_general(
        row_block, lift_matrix, (((1,), (1,)), ((), ())), preferred_element_type=jnp.float32
    )
    hidden = (jax.nn.silu(gate_value) * lift_value).astype(jnp.bfloat16)
    return jnp.dot(hidden, down_matrix, preferred_element_type=jnp.float32)


def retrace(action_values, actions, rewards, trace_codes):
    greedy = jnp.max(action_values, axis=1)
    picked = (
        actions[:, None] == jnp.arange(action_values.shape[1], dtype=jnp.int32)[None, :]
    ).astype(jnp.float32)
    taken = jnp.sum(action_values * picked, axis=1)
    trace = trace_codes.astype(jnp.float32) / 1024.0
    reward = rewards.astype(jnp.float32) * 0.25
    greedy = greedy.reshape(-1, STEPS)
    taken = taken.reshape(-1, STEPS)
    trace = trace.reshape(-1, STEPS)
    reward = reward.reshape(-1, STEPS)
    padding = jnp.zeros_like(greedy[:, :1])
    greedy_next = jnp.concatenate([greedy[:, 1:], padding], axis=1)
    taken_next = jnp.concatenate([taken[:, 1:], padding], axis=1)
    trace_next = jnp.concatenate([trace[:, 1:], padding], axis=1)
    driver = reward + DISCOUNT * (greedy_next - trace_next * taken_next)
    log_sums = jnp.cumsum(jnp.log(DISCOUNT * trace), axis=1)
    spans = log_sums[:, None, :] - log_sums[:, :, None]
    upper_mask = (
        jnp.arange(STEPS, dtype=jnp.int32)[None, :] >= jnp.arange(STEPS, dtype=jnp.int32)[:, None]
    )
    weight = jnp.where(upper_mask[None, :, :], jnp.exp(jnp.minimum(spans, 0.0)), 0.0)
    target = jnp.einsum("nts,ns->nt", weight, driver, precision=lax.Precision.HIGHEST)
    return target.reshape(-1)


def per_device(
    tokens,
    norm_gain,
    expert_ids,
    gate_codes,
    gate_weights,
    up_weights,
    down_weights,
    value_head,
    actions,
    rewards,
    trace_codes,
):
    groups = lax.axis_size("expert")
    tok_rows = tokens.shape[0]
    capacity = 2 * tok_rows * TOP // groups
    head_wide = value_head.astype(jnp.float32)
    flat_ids = expert_ids.reshape(-1)
    marked = (flat_ids[:, None] == jnp.arange(groups, dtype=jnp.int32)[None, :]).astype(jnp.int32)
    places = jnp.sum((jnp.cumsum(marked, axis=0) - 1) * marked, axis=1)
    slot_of = (flat_ids * capacity + places).reshape(tok_rows, TOP)
    slot_range = jnp.arange(groups * capacity, dtype=jnp.int32)
    matches = slot_of[None, :, :] == slot_range[:, None, None]
    dispatch_map = jnp.any(matches, axis=2).astype(jnp.bfloat16)
    outgoing = jnp.dot(dispatch_map, tokens, preferred_element_type=jnp.float32).astype(
        jnp.bfloat16
    )
    outgoing = outgoing.reshape(groups, capacity, tokens.shape[1])
    arrived = lax.all_to_all(outgoing, "expert", split_axis=0, concat_axis=0, tiled=True)
    arrived = lax.all_gather(arrived, "tensor", axis=2, tiled=True)
    row_count = groups * capacity
    row_block = arrived.reshape(row_count, arrived.shape[2])
    widened = row_block.astype(jnp.float32)
    scaling = lax.rsqrt(jnp.mean(widened * widened, axis=1, keepdims=True) + EPSILON)
    normed = (widened * scaling * norm_gain.astype(jnp.float32)[None, :]).astype(jnp.bfloat16)
    gathered = lax.all_gather(normed, "dp", axis=0, tiled=True)
    payload = lax.psum_scatter(
        expert_rows(gathered, gate_weights[0], up_weights[0], down_weights[0]),
        "dp",
        scatter_dimension=0,
        tiled=True,
    )
    returned = lax.all_to_all(
        payload.reshape(groups, capacity, payload.shape[1]),
        "expert",
        split_axis=0,
        concat_axis=0,
        tiled=True,
    )
    returned = returned.reshape(row_count, payload.shape[1])
    codes = gate_codes.astype(jnp.float32)
    gate_share = codes / jnp.sum(codes, axis=1, keepdims=True)
    combine_map = jnp.sum(jnp.where(matches, gate_share[None, :, :], 0.0), axis=2)
    blended = lax.dot_general(
        combine_map,
        returned,
        (((0,), (0,)), ((), ())),
        precision=lax.Precision.HIGHEST,
        preferred_element_type=jnp.float32,
    )
    partial_values = jnp.dot(
        blended, head_wide, precision=lax.Precision.HIGHEST, preferred_element_type=jnp.float32
    )
    action_values = lax.psum(partial_values, "tensor")
    retrace_targets = retrace(action_values, actions, rewards, trace_codes)
    return (action_values, retrace_targets)


def solution(mesh):
    in_specs = (
        P(("dp", "expert"), "tensor"),
        P(),
        P(("dp", "expert"), None),
        P(("dp", "expert"), None),
        P("expert", ("dp", "tensor"), None),
        P("expert", ("dp", "tensor"), None),
        P("expert", ("dp", "tensor"), None),
        P(),
        P(("dp", "expert")),
        P(("dp", "expert")),
        P(("dp", "expert")),
    )
    out_specs = (P(("dp", "expert"), None), P(("dp", "expert")))
    return jax.shard_map(
        per_device, mesh=mesh, in_specs=in_specs, out_specs=out_specs, check_vma=False
    )
```

profile of v0, /device:TPU:0, one launch (start us, length us, event | category | flops | bytes accessed | tf_op | source)
XLA Modules:
  0.0 473.5 jit_solution(6893080322555966808)
XLA Ops:
  7.2 0.8 copy.34
  8.1 0.1 eq.53
  8.2 0.1 eq.49
  8.4 1.2 reduce-window.14
  9.6 0.1 slice.20
  9.7 0.1 copy.36
  9.8 0.1 copy.37
  9.9 0.1 add_bitcast_fusion
  10.0 0.1 reduce_sum.48
  10.2 0.7 multiply_add_fusion
  11.0 1.4 convolution_convert_fusion
  12.4 32.0 %all_to_all.10 = bf16[4,128,1024]{2,1,0:T(8,128)(2,1)} all-to-all(bf16[4,128,1024]{2,1,0:T(8,128)(2,1)S(1)} %bitcast.62), channel_id=1, replica_groups=mesh['dp'=4,'expert'=4,'tensor'=2] {'expert'}, dimensions={0} | all-to-all | bytes 2097152 | tf_op jit(solution)/shard_map/all_to_all | solution.py:78
  44.4 9.8 %all-gather.3.cloned.1.call-done = bf16[4,128,2048]{2,1,0:T(8,128)(2,1)} async-done(((bf16[4,128,1024]{2,1,0:T(8,128)(2,1)}), bf16[4,128,2048]{2,1,0:T(8,128)(2,1)}) %all-gather.3.cloned.1.call-update) | async-done | bytes 2097168 | tf_op jit(solution)/shard_map/all_gather | solution.py:79
  54.2 2.1 multiply_reduce_fusion
  56.3 3.4 fusion.1
  59.7 0.2 reduce-scatter.2.cloned.1.call-start
  60.0 88.6 %all-gather.5.cloned.1.call-done = bf16[2048,2048]{1,0:T(8,128)(2,1)} async-done(((bf16[512,2048]{1,0:T(8,128)(2,1)}), bf16[2048,2048]{1,0:T(8,128)(2,1)}) %all-gather.5.cloned.1.call-update) | async-done | bytes 8388624 | tf_op jit(solution)/shard_map/all_gather | solution.py:85
  148.6 14.2 %fusion.6 = f32[2048,896]{1,0:T(8,128)} fusion(bf16[2048,2048]{1,0:T(8,128)(2,1)} %all-gather.5.cloned.1.call-done, bf16[1,896,2048]{2,1,0:T(8,128)(2,1)} %param.15), kind=kOutput, calls=%fused_computation.8 | convolution fusion | flops 7516192768 | bytes 19398656 | tf_op jit(solution)/shard_map/dot_general | solution.py:13
  162.8 26.7 %fusion.2 = f32[2048,2048]{1,0:T(8,128)} fusion(f32[2048,896]{1,0:T(8,128)} %fusion.6, bf16[2048,2048]{1,0:T(8,128)(2,1)} %all-gather.5.cloned.1.call-done, bf16[1,896,2048]{2,1,0:T(8,128)(2,1)} %param.17, bf16[1,896,2048]{2,1,0:T(8,128)(2,1)} %param.16), kind=kOutput, calls=%fused_computation.5 | convolution fusion | flops 15043395584 | bytes 39845888 | tf_op jit(solution)/shard_map/dot_general | solution.py:20
  189.5 153.9 %reduce-scatter.2.cloned.1.call-done = f32[512,2048]{1,0:T(8,128)} async-done(((f32[2048,2048]{1,0:T(8,128)}), f32[512,2048]{1,0:T(8,128)}) %reduce-scatter.2.cloned.1.call-update) | async-done | bytes 4194320 | tf_op jit(solution)/shard_map/reduce_scatter | solution.py:86
  343.4 5.0 %all-to-all-start.1 = ((f32[4,128,2048]{2,1,0:T(8,128)}), f32[4,128,2048]{2,1,0:T(8,128)}, u32[]{:S(2)}, u32[]{:S(2)}) async-start(f32[4,128,2048]{2,1,0:T(8,128)} %bitcast.61), calls=%async_computation.2 | async-start | bytes 8388608 | tf_op jit(solution)/shard_map/all_to_all | solution.py:92
  348.4 0.3 all-reduce.2.cloned.1.call-start
  348.8 92.9 %all-to-all-done.1 = f32[4,128,2048]{2,1,0:T(8,128)} async-done(((f32[4,128,2048]{2,1,0:T(8,128)}), f32[4,128,2048]{2,1,0:T(8,128)}, u32[]{:S(2)}, u32[]{:S(2)}) %all-to-all-start.1) | async-done | bytes 4194336 | tf_op jit(solution)/shard_map/all_to_all | solution.py:92
  441.7 4.6 fusion.34
  446.3 1.3 fusion.35
  447.6 0.1 copy.39
  447.8 0.2 reduce-window.19
  447.9 0.1 reduce.1
  448.0 15.5 %all-reduce.2.cloned.1.call-done = f32[128,128]{1,0:T(8,128)} async-done(((f32[128,128]{1,0:T(8,128)}), f32[128,128]{1,0:T(8,128)}) %all-reduce.2.cloned.1.call-update) | async-done | bytes 65552 | tf_op jit(solution)/shard_map/psum | solution.py:113
  463.6 1.0 select_reduce_fusion.1
  464.6 0.8 convolution_bitcast_fusion
  465.5 1.5 copy.43
  (32 shorter events, 0.6 us)
Async XLA Ops:
  7.2 439.1 %copy-start = (bf16[2048,128]{1,0:T(8,128)(2,1)S(1)}, bf16[2048,128]{1,0:T(8,128)(2,1)}, u32[]{:S(2)}) copy-start(bf16[2048,128]{1,0:T(8,128)(2,1)} %param.18) | copy-start | bytes 1572868
  7.2 37.2 %copy-start.1 = (bf16[2048]{0:T(1024)(128)(2,1)S(1)}, bf16[2048]{0:T(1024)(128)(2,1)}, u32[]{:S(2)}) copy-start(bf16[2048]{0:T(1024)(128)(2,1)} %param.12) | copy-start | bytes 12292
  7.2 47.0 %all-gather.3.cloned.1.call-start = ((), (), s32[]{:S(2)}) async-start(), calls=%async_computation.3 | async-start | bytes 3145728 | tf_op jit(solution)/shard_map/all_gather | solution.py:79
  44.4 104.2 %all-gather.5.cloned.1.call-start = ((), (), s32[]{:S(2)}) async-start(), calls=%async_computation.4 | async-start | bytes 10485760 | tf_op jit(solution)/shard_map/all_gather | solution.py:85
  59.7 283.6 %reduce-scatter.2.cloned.1.call-start = ((), (), s32[]{:S(2)}) async-start(), calls=%async_computation.5 | async-start | bytes 20971520 | tf_op jit(solution)/shard_map/reduce_scatter | solution.py:86
  343.4 5.3 %copy-start.2 = (s32[128,2]{0,1:T(2,128)S(1)}, s32[128,2]{0,1:T(2,128)}, u32[]{:S(2)}) copy-start(s32[128,2]{0,1:T(2,128)} %param.14) | copy-start | bytes 3076
  343.4 5.4 %copy-start.4 = (s32[128]{0:T(128)S(1)}, s32[128]{0:T(128)}, u32[]{:S(2)}) copy-start(s32[128]{0:T(128)} %param.21) | copy-start | bytes 1540
  343.4 98.3 %all-to-all-start.1 = ((f32[4,128,2048]{2,1,0:T(8,128)}), f32[4,128,2048]{2,1,0:T(8,128)}, u32[]{:S(2)}, u32[]{:S(2)}) async-start(f32[4,128,2048]{2,1,0:T(8,128)} %bitcast.61), calls=%async_computation.2 | async-start | bytes 8388608 | tf_op jit(solution)/shard_map/all_to_all | solution.py:92
  348.4 115.2 %copy-start.3 = (s32[128]{0:T(128)S(1)}, s32[128]{0:T(128)}, u32[]{:S(2)}) copy-start(s32[128]{0:T(128)} %param.19) | copy-start | bytes 1540
  348.4 116.2 %copy-start.5 = (s32[128]{0:T(128)S(1)}, s32[128]{0:T(128)}, u32[]{:S(2)}) copy-start(s32[128]{0:T(128)} %param.20) | copy-start | bytes 1540
  348.4 115.1 %all-reduce.2.cloned.1.call-start = ((), (), s32[]{:S(2)}) async-start(), calls=%async_computation.6 | async-start | bytes 131072 | tf_op jit(solution)/shard_map/psum | solution.py:113
Sparse Core Ops, SparseCore 0:
  44.5 9.6 all-gather.2
  59.9 88.6 all-gather.4
  189.6 153.7 reduce-scatter.1
  447.7 15.8 all-reduce.1
where the time goes:
time: 474 us; the launch traced here: 473 us
  waiting for transfers between devices  361 us (76%)
  matrix products  48.9 us (10%)
  blocking collectives  32 us (7%)
  between operations  13.9 us (3%)
  other arithmetic  9.03 us (2%)
  starting transfers between devices  5.55 us (1%)
    reduce_scatter x1, waiting for transfers between devices, per_device(): lax.psum_scatter(expert_rows(gathered, gate_weights[0], up_weights[0], do...  154 us
    all_to_all x1, waiting for transfers between devices, per_device(): lax.all_to_all(payload.reshape(groups, capacity, payload.shape[1]), 'expe...  92.9 us
    all_gather x1, waiting for transfers between devices, per_device(): gathered = lax.all_gather(normed, 'dp', axis=0, tiled=True)  88.6 us
    all_to_all x1, blocking collectives, per_device(): lax.all_to_all(outgoing, 'expert', split_axis=0, concat_axis=0, tiled=True)  32 us
    dot_general x1, matrix products, expert_rows(): return jnp.dot(hidden, down_matrix, preferred_element_type=jnp.float32)  26.7 us
    psum x1, waiting for transfers between devices, per_device(): action_values = lax.psum(partial_values, 'tensor')  15.5 us
    dot_general x1, matrix products, expert_rows(): lax.dot_general(row_block, gate_matrix, (((1,), (1,)), ((), ())), preferr...  14.2 us
    all_gather x1, waiting for transfers between devices, per_device(): arrived = lax.all_gather(arrived, 'tensor', axis=2, tiled=True)  9.76 us
  transfers between devices with their start and end apart: 5, of which 5 were waited for; matrix products, arithmetic and copies ran while one was open for 0% of the time, Pallas kernels for 0%

commit v1 on v0

--- a/solution.py
+++ b/solution.py
@@ -82,7 +82,8 @@
     widened = row_block.astype(jnp.float32)
     scaling = lax.rsqrt(jnp.mean(widened * widened, axis=1, keepdims=True) + EPSILON)
     normed = (widened * scaling * norm_gain.astype(jnp.float32)[None, :]).astype(jnp.bfloat16)
-    gathered = lax.all_gather(normed, "dp", axis=0, tiled=True)
+    outgoing_2 = jnp.stack([normed] * lax.axis_size("dp"))
+    gathered = jnp.concatenate(lax.all_to_all(outgoing_2, "dp", 0, 0), axis=0)
     payload = lax.psum_scatter(
         expert_rows(gathered, gate_weights[0], up_weights[0], down_weights[0]),
         "dp",

time: 474 us -> 482 us (1.017)
  blocking collectives: 32 us -> 129 us
  waiting for transfers between devices: 361 us -> 272 us
    all_to_all x0 -> x1, blocking collectives: none -> 97.2 us  [per_device(): gathered = jnp.concatenate(lax.all_to_all(outgoing_2, 'dp', 0, 0), axis=0)]
    all_gather x1 -> x0, waiting for transfers between devices: 88.6 us -> none  [per_device(): gathered = lax.all_gather(normed, 'dp', axis=0, tiled=True)]
  transfers between devices with their start and end apart: 5 -> 4, of which waited for: 5 -> 4; matrix products, arithmetic and copies ran while one was open for 0% -> 0% of each run, Pallas kernels for 0% -> 0%
where the time goes in v1:
time: 482 us; the launch traced here: 481 us
  waiting for transfers between devices  272 us (56%)
  blocking collectives  129 us (27%)
  matrix products  45.6 us (9%)
  between operations  13.9 us (3%)
  other arithmetic  7.73 us (2%)
  local copies, waits for them, and re-layouts  7.66 us (2%)
  starting transfers between devices  5.33 us (1%)
    reduce_scatter x1, waiting for transfers between devices, per_device(): lax.psum_scatter(expert_rows(gathered, gate_weights[0], up_weights[0], do...  153 us
    all_to_all x1, blocking collectives, per_device(): gathered = jnp.concatenate(lax.all_to_all(outgoing_2, 'dp', 0, 0), axis=0)  97.2 us
    all_to_all x1, waiting for transfers between devices, per_device(): lax.all_to_all(payload.reshape(groups, capacity, payload.shape[1]), 'expe...  92.9 us
    all_to_all x1, blocking collectives, per_device(): lax.all_to_all(outgoing, 'expert', split_axis=0, concat_axis=0, tiled=True)  32 us
    dot_general x1, matrix products, expert_rows(): return jnp.dot(hidden, down_matrix, preferred_element_type=jnp.float32)  26.7 us
    psum x1, waiting for transfers between devices, per_device(): action_values = lax.psum(partial_values, 'tensor')  15.6 us
    dot_general x1, matrix products, expert_rows(): lax.dot_general(row_block, gate_matrix, (((1,), (1,)), ((), ())), preferr...  10.9 us
    all_gather x1, waiting for transfers between devices, per_device(): arrived = lax.all_gather(arrived, 'tensor', axis=2, tiled=True)  9.76 us
  transfers between devices with their start and end apart: 4, of which 4 were waited for; matrix products, arithmetic and copies ran while one was open for 0% of the time, Pallas kernels for 0%

profile of v1, /device:TPU:0, one launch (start us, length us, event | category | flops | bytes accessed | tf_op | source)
XLA Modules:
  0.0 481.0 jit_solution(4002318857393006773)
XLA Ops:
  7.2 0.8 copy.34
  8.1 0.1 eq.53
  8.2 0.1 eq.49
  8.4 1.2 reduce-window.14
  9.7 0.1 copy.36
  9.8 0.1 copy.37
  9.9 0.1 add_bitcast_fusion
  10.0 0.1 reduce_sum.48
  10.2 0.7 multiply_add_fusion
  11.0 1.4 convolution_convert_fusion
  12.4 32.0 %all_to_all.15 = bf16[4,128,1024]{2,1,0:T(8,128)(2,1)} all-to-all(bf16[4,128,1024]{2,1,0:T(8,128)(2,1)S(1)} %bitcast.65), channel_id=1, replica_groups=mesh['dp'=4,'expert'=4,'tensor'=2] {'expert'}, dimensions={0} | all-to-all | bytes 2097152 | tf_op jit(solution)/shard_map/all_to_all | solution.py:78
  44.4 9.8 %all-gather.2.cloned.1.call-done = bf16[4,128,2048]{2,1,0:T(8,128)(2,1)} async-done(((bf16[4,128,1024]{2,1,0:T(8,128)(2,1)}), bf16[4,128,2048]{2,1,0:T(8,128)(2,1)}) %all-gather.2.cloned.1.call-update) | async-done | bytes 2097168 | tf_op jit(solution)/shard_map/all_gather | solution.py:79
  54.2 2.1 multiply_reduce_fusion
  56.3 2.1 fusion.1
  58.4 1.1 stack.2
  59.5 97.2 %all_to_all.16 = bf16[4,512,2048]{2,1,0:T(8,128)(2,1)S(1)} all-to-all(bf16[4,512,2048]{2,1,0:T(8,128)(2,1)S(1)} %stack.2), channel_id=1, replica_groups=mesh['dp'=4,'expert'=4,'tensor'=2] {'dp'}, dimensions={0} | all-to-all | bytes 16777216 | tf_op jit(solution)/shard_map/all_to_all | solution.py:86
  156.8 3.2 copy-done.1
  160.0 10.9 %fusion.6 = f32[2048,896]{1,0:T(8,128)} fusion(bf16[2048,2048]{1,0:T(8,128)(2,1)S(1)} %bitcast.62, bf16[1,896,2048]{2,1,0:T(8,128)(2,1)S(1)} %copy-done.5), kind=kOutput, calls=%fused_computation.8 | convolution fusion | flops 7516192768 | bytes 19398656 | tf_op jit(solution)/shard_map/dot_general | solution.py:13
  170.9 26.7 %fusion.2 = f32[2048,2048]{1,0:T(8,128)} fusion(f32[2048,896]{1,0:T(8,128)} %fusion.6, bf16[2048,2048]{1,0:T(8,128)(2,1)} %bitcast.63, bf16[1,896,2048]{2,1,0:T(8,128)(2,1)} %param.17, bf16[1,896,2048]{2,1,0:T(8,128)(2,1)} %param.16), kind=kOutput, calls=%fused_computation.5 | convolution fusion | flops 15043395584 | bytes 39845888 | tf_op jit(solution)/shard_map/dot_general | solution.py:20
  197.6 153.3 %reduce-scatter.2.cloned.1.call-done = f32[512,2048]{1,0:T(8,128)} async-done(((f32[2048,2048]{1,0:T(8,128)}), f32[512,2048]{1,0:T(8,128)}) %reduce-scatter.2.cloned.1.call-update) | async-done | bytes 4194320 | tf_op jit(solution)/shard_map/reduce_scatter | solution.py:87
  350.9 5.0 %all-to-all-start.2 = ((f32[4,128,2048]{2,1,0:T(8,128)}), f32[4,128,2048]{2,1,0:T(8,128)}, u32[]{:S(2)}, u32[]{:S(2)}) async-start(f32[4,128,2048]{2,1,0:T(8,128)} %bitcast.64), calls=%async_computation.3 | async-start | bytes 8388608 | tf_op jit(solution)/shard_map/all_to_all | solution.py:93
  356.0 0.3 all-reduce.2.cloned.1.call-start
  356.4 92.9 %all-to-all-done.2 = f32[4,128,2048]{2,1,0:T(8,128)} async-done(((f32[4,128,2048]{2,1,0:T(8,128)}), f32[4,128,2048]{2,1,0:T(8,128)}, u32[]{:S(2)}, u32[]{:S(2)}) %all-to-all-start.2) | async-done | bytes 4194336 | tf_op jit(solution)/shard_map/all_to_all | solution.py:93
  449.3 4.5 fusion.34
  453.8 1.3 fusion.35
  455.1 0.1 copy.39
  455.3 0.2 reduce-window.19
  455.4 0.1 reduce.1
  455.5 15.6 %all-reduce.2.cloned.1.call-done = f32[128,128]{1,0:T(8,128)} async-done(((f32[128,128]{1,0:T(8,128)}), f32[128,128]{1,0:T(8,128)}) %all-reduce.2.cloned.1.call-update) | async-done | bytes 65552 | tf_op jit(solution)/shard_map/psum | solution.py:114
  471.1 1.0 select_reduce_fusion.1
  472.2 0.8 convolution_bitcast_fusion
  473.0 1.5 copy.43
  (35 shorter events, 0.7 us)
Async XLA Ops:
  7.2 446.6 %copy-start = (bf16[2048,128]{1,0:T(8,128)(2,1)S(1)}, bf16[2048,128]{1,0:T(8,128)(2,1)}, u32[]{:S(2)}) copy-start(bf16[2048,128]{1,0:T(8,128)(2,1)} %param.18) | copy-start | bytes 1572868
  7.2 37.2 %copy-start.2 = (bf16[2048]{0:T(1024)(128)(2,1)S(1)}, bf16[2048]{0:T(1024)(128)(2,1)}, u32[]{:S(2)}) copy-start(bf16[2048]{0:T(1024)(128)(2,1)} %param.12) | copy-start | bytes 12292
  7.2 47.0 %all-gather.2.cloned.1.call-start = ((), (), s32[]{:S(2)}) async-start(), calls=%async_computation.4 | async-start | bytes 3145728 | tf_op jit(solution)/shard_map/all_gather | solution.py:79
  44.4 306.6 %reduce-scatter.2.cloned.1.call-start = ((), (), s32[]{:S(2)}) async-start(), calls=%async_computation.5 | async-start | bytes 20971520 | tf_op jit(solution)/shard_map/reduce_scatter | solution.py:87
  59.5 100.5 %copy-start.5 = (bf16[1,896,2048]{2,1,0:T(8,128)(2,1)S(1)}, bf16[1,896,2048]{2,1,0:T(8,128)(2,1)}, u32[]{:S(2)}) copy-start(bf16[1,896,2048]{2,1,0:T(8,128)(2,1)} %param.15) | copy-start | bytes 11010052
  156.8 3.2 copy-start.1
  350.9 5.3 %copy-start.3 = (s32[128,2]{0,1:T(2,128)S(1)}, s32[128,2]{0,1:T(2,128)}, u32[]{:S(2)}) copy-start(s32[128,2]{0,1:T(2,128)} %param.14) | copy-start | bytes 3076
  350.9 5.4 %copy-start.6 = (s32[128]{0:T(128)S(1)}, s32[128]{0:T(128)}, u32[]{:S(2)}) copy-start(s32[128]{0:T(128)} %param.21) | copy-start | bytes 1540
  350.9 98.3 %all-to-all-start.2 = ((f32[4,128,2048]{2,1,0:T(8,128)}), f32[4,128,2048]{2,1,0:T(8,128)}, u32[]{:S(2)}, u32[]{:S(2)}) async-start(f32[4,128,2048]{2,1,0:T(8,128)} %bitcast.64), calls=%async_computation.3 | async-start | bytes 8388608 | tf_op jit(solution)/shard_map/all_to_all | solution.py:93
  355.9 115.2 %copy-start.4 = (s32[128]{0:T(128)S(1)}, s32[128]{0:T(128)}, u32[]{:S(2)}) copy-start(s32[128]{0:T(128)} %param.19) | copy-start | bytes 1540
  355.9 116.2 %copy-start.7 = (s32[128]{0:T(128)S(1)}, s32[128]{0:T(128)}, u32[]{:S(2)}) copy-start(s32[128]{0:T(128)} %param.20) | copy-start | bytes 1540
  356.0 115.1 %all-reduce.2.cloned.1.call-start = ((), (), s32[]{:S(2)}) async-start(), calls=%async_computation.6 | async-start | bytes 131072 | tf_op jit(solution)/shard_map/psum | solution.py:114
Sparse Core Ops, SparseCore 0:
  44.5 9.6 all-gather.1
  197.7 153.1 reduce-scatter.1
  455.2 15.8 all-reduce.1
